TPU v7x, 32 devices: a whole 2x2x4 slice. The times are simulated.
32 devices in a mesh: dp: 8 (over y, x, core), expert: 4 (over z).
Axes of the slice: x: 2, y: 2, z: 4, core: 2. Of those that a mesh axis runs over, the one named last changes fastest.
Arguments:
- tokens: bfloat16 [4096, 4096], P(('dp', 'expert')), may hold values from -6 to 6
- probs: bfloat16 [4096, 1], P(('dp', 'expert')), may hold values from 0.19921875 to 1
- routes: int32 [4096, 1], P(('dp', 'expert')), may hold values from 0 to 3; in each aligned block of 128 rows (0 to 127, 128 to 255, ...) at most 34 rows name the same one
- w_gate: bfloat16 [4, 4096, 1024], P('expert', 'dp'), may hold values from -0.09375 to 0.09375
- w_up: bfloat16 [4, 4096, 1024], P('expert', 'dp'), may hold values from -0.09375 to 0.09375
- w_down: bfloat16 [4, 1024, 4096], P('expert', None, 'dp'), may hold values from -0.1875 to 0.1875
- cotangent: bfloat16 [4096, 4096], P(('dp', 'expert')), may hold values from -6 to 6
Outputs:
- mixed: bfloat16 [4096, 4096], P(('dp', 'expert'))
- input_grad: bfloat16 [4096, 4096], P(('dp', 'expert'))
- grad_gate: bfloat16 [4, 4096, 1024], P('expert', 'dp')
- grad_up: bfloat16 [4, 4096, 1024], P('expert', 'dp')
- grad_down: bfloat16 [4, 1024, 4096], P('expert', None, 'dp')
Inputs may be any that keep to these rules, and one draw needn't show every extreme that they name: `routes`: each row names exactly one expert. Among the 128 rows of one device (aligned blocks), no expert is named more than 34 times, a bound that some block reaches.
All inputs are finite; a program needn't handle non-finite values.
Results may differ from a plain program's by a relative error of at most 0.025.
Values may be sent and summed in bfloat16 or wider, within the bound.
A program may use at most 128 MiB of HBM per device.

v0:
```python
import jax
import jax.numpy as jnp
from jax import lax
from jax.sharding import PartitionSpec as P


def slot_table(routes, experts_all, capacity):
    flat = routes.reshape(-1)
    hits = (flat[:, None] == jnp.arange(experts_all, dtype=jnp.int32)[None, :]).astype(jnp.int32)
    before = jnp.cumsum(hits, axis=0) - hits
    place = jnp.sum(before * hits, axis=1)
    target = flat * capacity + place
    table = jnp.arange(experts_all * capacity, dtype=jnp.int32)[:, None] == target[None, :]
    return table.astype(jnp.bfloat16)


def spread_rows(table, values, slices):
    shaped = values.reshape(values.shape[0], slices, values.shape[1] // slices)
    return jnp.einsum("st,tnk->nsk", table, shaped, preferred_element_type=jnp.float32).astype(
        jnp.bfloat16
    )


def to_rows(received, local_count):
    sources, slots, width = received.shape
    shaped = received.reshape(sources, local_count, slots // local_count, width)
    shaped = jnp.swapaxes(shaped, 1, 2)
    return shaped.reshape(sources * (slots // local_count), local_count, width)


def to_sources(rowwise, capacity):
    total, local_count, width = rowwise.shape
    shaped = rowwise.reshape(total // capacity, capacity, local_count, width)
    shaped = jnp.swapaxes(shaped, 1, 2)
    return shaped.reshape(total // capacity, local_count * capacity, width)


def collect(table, back, tok_rows, top):
    picked = jnp.einsum("st,nsk->tnk", table, back, preferred_element_type=jnp.float32)
    return picked.reshape(tok_rows, top, -1)


def per_device(tokens, probs, routes, w_gate, w_up, w_down, cotangent):
    local_count = w_gate.shape[0]
    n_dp = lax.axis_size("dp")
    n_exp = lax.axis_size("expert")
    experts_all = local_count * n_exp
    tok_rows, width = tokens.shape
    top = routes.shape[1]
    capacity = max(2, 17 * tok_rows * top // (16 * experts_all))
    blocks = n_dp * n_exp
    slot_width = width // n_dp
    table = slot_table(routes, experts_all, capacity)
    x_send = spread_rows(table, jnp.repeat(tokens, top, axis=0), n_dp)
    x_send = x_send.reshape(blocks, local_count * capacity, slot_width)
    weight = probs.astype(jnp.float32)
    scaled = (jnp.repeat(cotangent, top, axis=0).astype(jnp.float32) * weight).astype(jnp.bfloat16)
    x_got = lax.all_to_all(x_send, ("dp", "expert"), split_axis=0, concat_axis=0, tiled=True)
    rows = to_rows(x_got, local_count)
    part = rows
    gate = jnp.einsum("red,edf->ref", part, w_gate, preferred_element_type=jnp.float32)
    upper = jnp.einsum("red,edf->ref", part, w_up, preferred_element_type=jnp.float32)
    summed = lax.psum_scatter(
        jnp.stack([gate, upper], axis=2).astype(jnp.bfloat16), "dp", scatter_dimension=0, tiled=True
    ).astype(jnp.float32)
    gate_pre = summed[:, :, 0]
    up_value = summed[:, :, 1]
    sig = jax.nn.sigmoid(gate_pre)
    act = (gate_pre * sig * up_value).astype(jnp.bfloat16)
    act_all = lax.all_gather(act, "dp", axis=0, tiled=True)
    result = jnp.einsum("ref,efd->red", act_all, w_down, preferred_element_type=jnp.float32).astype(
        jnp.bfloat16
    )
    outgoing = to_sources(result, capacity)
    back = lax.all_to_all(outgoing, ("dp", "expert"), split_axis=0, concat_axis=0, tiled=True)
    back = back.reshape(n_dp, experts_all * capacity, slot_width)
    picked = collect(table, back, tok_rows, top)
    mixed = jnp.sum(picked * weight[..., None], axis=1).astype(jnp.bfloat16)
    dy_send = spread_rows(table, scaled, n_dp).reshape(blocks, local_count * capacity, slot_width)
    dy_got = lax.all_to_all(dy_send, ("dp", "expert"), split_axis=0, concat_axis=0, tiled=True)
    dout = to_rows(dy_got, local_count)
    grad_down = jnp.einsum("ref,red->efd", act_all, dout, preferred_element_type=jnp.float32)
    part = dout
    dact = lax.psum_scatter(
        jnp.einsum("red,efd->ref", part, w_down, preferred_element_type=jnp.float32).astype(
            jnp.bfloat16
        ),
        "dp",
        scatter_dimension=0,
        tiled=True,
    ).astype(jnp.float32)
    dgate = (dact * up_value * sig * (1.0 + gate_pre * (1.0 - sig))).astype(jnp.bfloat16)
    dup = (dact * gate_pre * sig).astype(jnp.bfloat16)
    dgate_all, dup_all = (
        lax.all_gather(dgate, "dp", axis=0, tiled=True),
        lax.all_gather(dup, "dp", axis=0, tiled=True),
    )
    grad_gate = jnp.einsum("red,ref->edf", rows, dgate_all, preferred_element_type=jnp.float32)
    grad_up = jnp.einsum("red,ref->edf", rows, dup_all, preferred_element_type=jnp.float32)
    slot_grad = jnp.einsum(
        "ref,edf->red", dgate_all, w_gate, preferred_element_type=jnp.float32
    ) + jnp.einsum("ref,edf->red", dup_all, w_up, preferred_element_type=jnp.float32)
    slot_grad = slot_grad.astype(jnp.bfloat16)
    returned = lax.all_to_all(
        to_sources(slot_grad, capacity), ("dp", "expert"), split_axis=0, concat_axis=0, tiled=True
    )
    returned = returned.reshape(n_dp, experts_all * capacity, slot_width)
    input_grad = jnp.sum(collect(table, returned, tok_rows, top), axis=1).astype(jnp.bfloat16)
    return (
        mixed,
        input_grad,
        grad_gate.astype(jnp.bfloat16),
        grad_up.astype(jnp.bfloat16),
        grad_down.astype(jnp.bfloat16),
    )


def solution(mesh):
    return jax.shard_map(
        per_device,
        mesh=mesh,
        in_specs=(
            P(("dp", "expert"), None),
            P(("dp", "expert"), None),
            P(("dp", "expert"), None),
            P("expert", "dp", None),
            P("expert", "dp", None),
            P("expert", None, "dp"),
            P(("dp", "expert"), None),
        ),
        out_specs=(
            P(("dp", "expert"), None),
            P(("dp", "expert"), None),
            P("expert", "dp", None),
            P("expert", "dp", None),
            P("expert", None, "dp"),
        ),
        check_vma=False,
    )
```

profile of v0, /device:TPU:25, one launch (start us, length us, event | category | flops | bytes accessed | tf_op | source)
XLA Modules:
  0.0 322.1 jit_solution(5524149168156521085)
XLA Ops:
  8.2 0.8 select_reduce_fusion
  9.7 1.7 fusion.26
  11.7 35.9 %all_to_all.20 = bf16[32,34,512]{2,1,0:T(8,128)(2,1)} all-to-all(bf16[32,34,512]{2,1,0:T(8,128)(2,1)S(1)} %reshape.232), channel_id=1, replica_groups=mesh['dp'=8,'expert'=4] {'dp','expert'}, dimensions={0} | all-to-all | bytes 2228224 | tf_op jit(solution)/shard_map/all_to_all | solution.py:58
  47.7 1.5 reshape.233
  49.1 1.3 fusion.1
  50.8 1.3 fusion.2
  52.5 9.6 %copy.22 = bf16[1088,1,2,1024]{3,2,1,0:T(2,128)(2,1)S(1)} copy(bf16[1088,1,2,1024]{3,0,2,1:T(8,128)(2,1)S(1)} %pad_maximum_fusion) | data formatting | bytes 8912896
  62.1 3.9 %copy.28 = bf16[136,8,2,1024]{3,1,2,0:T(8,128)(2,1)} copy(bf16[136,8,2,1024]{3,2,1,0:T(2,128)(2,1)S(1)} %bitcast.140) | data formatting | bytes 8912896
  68.3 35.3 %all_to_all.21 = bf16[32,34,512]{2,1,0:T(8,128)(2,1)} all-to-all(bf16[32,34,512]{2,1,0:T(8,128)(2,1)S(1)} %reshape.240), channel_id=1, replica_groups=mesh['dp'=8,'expert'=4] {'dp','expert'}, dimensions={0} | all-to-all | bytes 2228224 | tf_op jit(solution)/shard_map/all_to_all | solution.py:80
  103.6 1.5 reshape.241
  105.1 2.8 fusion.3
  107.9 14.6 %reduce-scatter.7.cloned.1.call-done = bf16[136,2048]{1,0:T(8,128)(2,1)} async-done(((bf16[1088,2048]{1,0:T(8,128)(2,1)}), bf16[136,2048]{1,0:T(8,128)(2,1)}) %reduce-scatter.7.cloned.1.call-update) | async-done | bytes 557072
  122.5 2.3 reshape.249
  124.9 42.7 %reduce-scatter.5.cloned.1.call-done = bf16[136,1,1024]{2,0,1:T(8,128)(2,1)} async-done(((bf16[1088,1,1024]{2,0,1:T(8,128)(2,1)}), bf16[136,1,1024]{2,0,1:T(8,128)(2,1)}) %reduce-scatter.5.cloned.1.call-update) | async-done | bytes 278544 | tf_op jit(solution)/shard_map/reduce_scatter | solution.py:84
  167.7 2.2 fusion.51
  171.1 28.0 %all-gather.6.cloned.1.call-done = bf16[1088,1,1024]{2,0,1:T(8,128)(2,1)} async-done(((bf16[136,1,1024]{2,0,1:T(8,128)(2,1)}), bf16[1088,1,1024]{2,0,1:T(8,128)(2,1)}) %all-gather.6.cloned.1.call-update) | async-done | bytes 2228240 | tf_op jit(solution)/shard_map/all_gather | solution.py:95
  199.1 4.4 %fusion.12 = f32[1088,512]{1,0:T(8,128)} fusion(bf16[1088,1,1024]{2,0,1:T(8,128)(2,1)} %all-gather.6.cloned.1.call-done, bf16[1,512,1024]{2,1,0:T(8,128)(2,1)S(1)} %copy-done), kind=kOutput, calls=%fused_computation.20 | convolution fusion | flops 1140850688 | bytes 5505024 | tf_op jit(solution)/shard_map/ref,edf->red/dot_general | solution.py:100
  203.5 26.3 %all-gather.8.cloned.1.call-done = bf16[1088,1,1024]{2,0,1:T(8,128)(2,1)} async-done(((bf16[136,1,1024]{2,0,1:T(8,128)(2,1)}), bf16[1088,1,1024]{2,0,1:T(8,128)(2,1)}) %all-gather.8.cloned.1.call-update) | async-done | bytes 2228240 | tf_op jit(solution)/shard_map/all_gather | solution.py:96
  229.7 3.7 %fusion.6 = bf16[1088,1,512]{2,0,1:T(8,128)(2,1)S(1)} fusion(f32[1088,512]{1,0:T(8,128)} %fusion.12, bf16[1088,1,1024]{2,0,1:T(8,128)(2,1)} %all-gather.8.cloned.1.call-done, bf16[1,512,1024]{2,1,0:T(8,128)(2,1)S(1)} %copy-done.9), kind=kOutput, calls=%fused_computation.14 | convolution fusion | flops 1141964800 | bytes 6619136 | tf_op jit(solution)/shard_map/ref,edf->red/dot_general | solution.py:102
  233.4 1.3 reshape_transpose_reshape.9
  234.8 4.8 %all-to-all-start.3 = ((bf16[32,34,512]{2,1,0:T(8,128)(2,1)}), bf16[32,34,512]{2,1,0:T(8,128)(2,1)S(1)}, u32[]{:S(2)}, u32[]{:S(2)}) async-start(bf16[32,34,512]{2,1,0:T(8,128)(2,1)} %reshape_transpose_reshape.9), calls=%async_computation.4 | async-start | bytes 2621440 | tf_op jit(solution)/shard_map/all_to_all | solution.py:104
  239.5 32.7 %all-gather.4.cloned.1.call-done = bf16[1088,1,1024]{2,0,1:T(8,128)(2,1)} async-done(((bf16[136,1,1024]{2,0,1:T(8,128)(2,1)}), bf16[1088,1,1024]{2,0,1:T(8,128)(2,1)}) %all-gather.4.cloned.1.call-update) | async-done | bytes 2228240 | tf_op jit(solution)/shard_map/all_gather | solution.py:70
  272.2 4.0 %fusion.5 = bf16[1088,1,512]{2,0,1:T(8,128)(2,1)} fusion(bf16[1088,1,1024]{2,0,1:T(8,128)(2,1)} %all-gather.4.cloned.1.call-done, bf16[1,1024,512]{2,1,0:T(8,128)(2,1)S(1)} %copy-done.11), kind=kOutput, calls=%fused_computation.13 | convolution fusion | flops 1141407744 | bytes 4390912 | tf_op jit(solution)/shard_map/ref,efd->red/dot_general | solution.py:71
  276.2 2.4 reshape_transpose_reshape.8
  278.6 4.9 %all-to-all-start.1 = ((bf16[32,34,512]{2,1,0:T(8,128)(2,1)}), bf16[32,34,512]{2,1,0:T(8,128)(2,1)}, u32[]{:S(2)}, u32[]{:S(2)}) async-start(bf16[32,34,512]{2,1,0:T(8,128)(2,1)} %reshape_transpose_reshape.8), calls=%async_computation.1 | async-start | bytes 2621440 | tf_op jit(solution)/shard_map/all_to_all | solution.py:75
  283.6 4.3 %fusion.28 = bf16[1,512,1024]{2,1,0:T(8,128)(2,1)} fusion(bf16[1088,512]{1,0:T(8,128)(2,1)S(1)} %copy-done.2, bf16[1088,1,1024]{2,0,1:T(8,128)(2,1)} %all-gather.8.cloned.1.call-done), kind=kOutput, calls=%fused_computation.33 | convolution fusion | flops 1141374976 | bytes 4390912 | tf_op jit(solution)/shard_map/red,ref->edf/dot_general | solution.py:99
  287.9 2.5 fusion.31
  290.4 2.5 fusion.34
  293.4 1.5 convolution_convert_fusion
  294.9 17.5 %all-to-all-done.1 = bf16[32,34,512]{2,1,0:T(8,128)(2,1)} async-done(((bf16[32,34,512]{2,1,0:T(8,128)(2,1)}), bf16[32,34,512]{2,1,0:T(8,128)(2,1)}, u32[]{:S(2)}, u32[]{:S(2)}) %all-to-all-start.1) | async-done | bytes 1114144 | tf_op jit(solution)/shard_map/all_to_all | solution.py:75
  312.5 1.5 reshape.238
  314.0 1.5 fusion
  (50 shorter events, 7.0 us)
Async XLA Ops:
  7.2 42.0 %copy-start = (bf16[1,512,1024]{2,1,0:T(8,128)(2,1)S(1)}, bf16[1,512,1024]{2,1,0:T(8,128)(2,1)}, u32[]{:S(2)}) copy-start(bf16[1,512,1024]{2,1,0:T(8,128)(2,1)} %param.10) | copy-start | bytes 3145732
  7.2 115.3 %reduce-scatter.7.cloned.1.call-start = ((), (), s32[]{:S(2)}) async-start(), calls=%async_computation.10 | async-start | bytes 5013504
  49.1 1.4 copy-start.1
  49.1 1.6 copy-start.8
  66.0 0.7 copy-start.12
  66.0 1.2 copy-start.5
  66.0 101.7 %reduce-scatter.5.cloned.1.call-start = ((), (), s32[]{:S(2)}) async-start(), calls=%async_computation.7 | async-start | bytes 2506752 | tf_op jit(solution)/shard_map/reduce_scatter | solution.py:84
  68.3 36.8 %copy-start.10 = (bf16[1,1024,512]{2,1,0:T(8,128)(2,1)S(1)}, bf16[1,1024,512]{2,1,0:T(8,128)(2,1)}, u32[]{:S(2)}) copy-start(bf16[1,1024,512]{2,1,0:T(8,128)(2,1)} %param.12) | copy-start | bytes 3145732
  105.1 2.8 copy-start.3
  107.9 91.2 %all-gather.6.cloned.1.call-start = ((), (), s32[]{:S(2)}) async-start(), calls=%async_computation.8 | async-start | bytes 2506752 | tf_op jit(solution)/shard_map/all_gather | solution.py:95
  169.9 59.8 %all-gather.8.cloned.1.call-start = ((), (), s32[]{:S(2)}) async-start(), calls=%async_computation.9 | async-start | bytes 2506752 | tf_op jit(solution)/shard_map/all_gather | solution.py:96
  170.5 101.8 %all-gather.4.cloned.1.call-start = ((), (), s32[]{:S(2)}) async-start(), calls=%async_computation.6 | async-start | bytes 2506752 | tf_op jit(solution)/shard_map/all_gather | solution.py:70
  171.0 58.7 %copy-start.9 = (bf16[1,512,1024]{2,1,0:T(8,128)(2,1)S(1)}, bf16[1,512,1024]{2,1,0:T(8,128)(2,1)}, u32[]{:S(2)}) copy-start(bf16[1,512,1024]{2,1,0:T(8,128)(2,1)} %param.11) | copy-start | bytes 3145732
  233.4 38.9 %copy-start.11 = (bf16[1,1024,512]{2,1,0:T(8,128)(2,1)S(1)}, bf16[1,1024,512]{2,1,0:T(8,128)(2,1)}, u32[]{:S(2)}) copy-start(bf16[1,1024,512]{2,1,0:T(8,128)(2,1)} %param.12) | copy-start | bytes 3145732
  234.8 43.9 %all-to-all-start.3 = ((bf16[32,34,512]{2,1,0:T(8,128)(2,1)}), bf16[32,34,512]{2,1,0:T(8,128)(2,1)S(1)}, u32[]{:S(2)}, u32[]{:S(2)}) async-start(bf16[32,34,512]{2,1,0:T(8,128)(2,1)} %reshape_transpose_reshape.9), calls=%async_computation.4 | async-start | bytes 2621440 | tf_op jit(solution)/shard_map/all_to_all | solution.py:104
  276.2 7.3 %copy-start.2 = (bf16[1088,512]{1,0:T(8,128)(2,1)S(1)}, bf16[1088,512]{1,0:T(8,128)(2,1)}, u32[]{:S(2)}) copy-start(bf16[1088,512]{1,0:T(8,128)(2,1)} %copy-done.1) | copy-start | bytes 3342340
  278.6 33.8 %all-to-all-start.1 = ((bf16[32,34,512]{2,1,0:T(8,128)(2,1)}), bf16[32,34,512]{2,1,0:T(8,128)(2,1)}, u32[]{:S(2)}, u32[]{:S(2)}) async-start(bf16[32,34,512]{2,1,0:T(8,128)(2,1)} %reshape_transpose_reshape.8), calls=%async_computation.1 | async-start | bytes 2621440 | tf_op jit(solution)/shard_map/all_to_all | solution.py:75
  283.6 4.3 %copy-start.6 = (bf16[1088,1,1024]{2,0,1:T(8,128)(2,1)S(1)}, bf16[1088,1,1024]{2,0,1:T(8,128)(2,1)}, u32[]{:S(2)}) copy-start(bf16[1088,1,1024]{2,0,1:T(8,128)(2,1)} %all-gather.6.cloned.1.call-done) | copy-start | bytes 6684676
  287.9 2.5 copy-start.4
  287.9 2.5 copy-start.7
Sparse Core Ops, SparseCore 0:
  66.1 56.3 reduce-scatter.6
  125.8 41.7 reduce-scatter.4
  170.1 28.8 all-gather.5
  201.4 28.3 all-gather.7
  232.0 40.1 all-gather.3
where the time goes:
time: 327 us; the launch traced here: 322 us
  waiting for transfers between devices  163 us (50%)
  blocking collectives  71.2 us (22%)
  matrix products  32 us (10%)
  local copies, waits for them, and re-layouts  26.6 us (8%)
  between operations  14.1 us (4%)
  starting transfers between devices  10.1 us (3%)
  other arithmetic  5.48 us (2%)
    reduce_scatter x1, waiting for transfers between devices, per_device(): lax.psum_scatter(jnp.einsum('red,efd->ref', part, w_down, preferred_eleme...  42.7 us
    all_to_all x1, blocking collectives, per_device(): lax.all_to_all(x_send, ('dp', 'expert'), split_axis=0, concat_axis=0, til...  35.9 us
    all_to_all x1, blocking collectives, per_device(): lax.all_to_all(dy_send, ('dp', 'expert'), split_axis=0, concat_axis=0, ti...  35.3 us
    all_gather x1, waiting for transfers between devices, per_device(): act_all = lax.all_gather(act, 'dp', axis=0, tiled=True)  32.7 us
    all_gather x1, waiting for transfers between devices, per_device(): lax.all_gather(dgate, 'dp', axis=0, tiled=True)  28 us
    all_gather x1, waiting for transfers between devices, per_device(): lax.all_gather(dup, 'dp', axis=0, tiled=True)  26.3 us
    all_to_all x1, waiting for transfers between devices, per_device(): lax.all_to_all(outgoing, ('dp', 'expert'), split_axis=0, concat_axis=0, t...  17.5 us
    unnamed x29, local copies, waits for them, and re-layouts  17.2 us
  transfers between devices with their start and end apart: 7, of which 6 were waited for; matrix products, arithmetic and copies ran while one was open for 11% of the time, Pallas kernels for 0%

commit v1 on v0

--- a/solution.py
+++ b/solution.py
@@ -1,7 +1,419 @@
+import functools
+
 import jax
 import jax.numpy as jnp
 from jax import lax
+from jax.experimental import pallas as pl
+from jax.experimental.pallas import tpu as pltpu
 from jax.sharding import PartitionSpec as P
+
+BF = jnp.bfloat16
+F32 = jnp.float32
+
+
+def nn(a, b):
+    return lax.dot_general(a, b, (((1,), (0,)), ((), ())), preferred_element_type=F32)
+
+
+def nt(a, b):
+    return lax.dot_general(a, b, (((1,), (1,)), ((), ())), preferred_element_type=F32)
+
+
+def tn(a, b):
+    return lax.dot_general(a, b, (((0,), (0,)), ((), ())), preferred_element_type=F32)
+
+
+def layer_kernel(
+    n, e_n, cap,
+    tok, dys, tgt, wg, wu, wd,
+    res_o, ig_o, gg_o, gu_o, gd_o,
+    tga, table, xa, da, xs, ds_, xr, dr, xp, dp, pwg, pwu, pwd,
+    gs, gr, hs, hr, pre, upv, act, dga, dua, rs, rr, ss, sr, un, un2, x_t,
+    sem_dp, sem_pw, sem_ex, sem_q,
+):
+    m = lax.axis_index("dp")
+    z = lax.axis_index("expert")
+    q_n = n // 2
+    q = m // 2
+    c = lax.rem(m, 2)
+    pm = m + 1 - 2 * c
+    slots = n * cap
+    t_rows, w = tok.shape[0], tok.shape[1] // n
+    ff = wg.shape[1]
+    fh = ff // 2
+    b = fh // q_n
+
+    def rows(k):
+        return pl.ds(pl.multiple_of(k * slots, 16), slots)
+
+    def toks(k):
+        return pl.ds(pl.multiple_of(k * t_rows, 128), t_rows)
+
+    def cols(k):
+        return pl.ds(pl.multiple_of(k * w, 128), w)
+
+    my_half = pl.ds(pl.multiple_of(c * fh, 128), fh)
+    other_half = pl.ds(pl.multiple_of((1 - c) * fh, 128), fh)
+
+    def block(qq):
+        return pl.ds(pl.multiple_of(c * fh + qq * b, 128), b)
+
+    def copy(src, dst, send, recv, dp_at, ex_at):
+        return pltpu.make_async_remote_copy(
+            src_ref=src, dst_ref=dst, send_sem=send, recv_sem=recv,
+            device_id=(dp_at, ex_at), device_id_type=pl.DeviceIdType.MESH,
+        )
+
+    def dp_pair(no, src, dst):
+        def out(i):
+            return copy(src(i), dst(m), sem_dp.at[2 * no, i], sem_dp.at[2 * no + 1, m], i, z)
+
+        def got(i):
+            return copy(src(i), dst(i), sem_dp.at[2 * no, i], sem_dp.at[2 * no + 1, i], i, z)
+
+        return out, got
+
+    def ex_pair(no, src, dst):
+        def out(i):
+            return copy(src.at[rows(i)], dst.at[rows(z)], sem_ex.at[2 * no, i], sem_ex.at[2 * no + 1, z], m, i)
+
+        def got(i):
+            return copy(src.at[rows(i)], dst.at[rows(i)], sem_ex.at[2 * no, i], sem_ex.at[2 * no + 1, i], m, i)
+
+        return out, got
+
+    def pass_pair(no, src, dst):
+        def out(k):
+            return copy(src(k), src(k) if dst is None else dst(k), sem_ex.at[2 * no, k], sem_ex.at[2 * no + 1, k], pm, z)
+
+        return out
+
+    def q_pair(no, src, dst):
+        def out(k, i):
+            return copy(src(k, i), dst(k, q), sem_q.at[2 * no, k, i], sem_q.at[2 * no + 1, k, q], 2 * i + c, z)
+
+        def got(k, i):
+            return copy(src(k, i), dst(k, i), sem_q.at[2 * no, k, i], sem_q.at[2 * no + 1, k, i], 2 * i + c, z)
+
+        return out, got
+
+    tg_out, tg_got = dp_pair(0, lambda i: tgt, lambda i: tga.at[i])
+    xa_out, xa_got = dp_pair(1, lambda i: tok.at[:, cols(i)], lambda i: xa.at[toks(i)])
+    da_out, da_got = dp_pair(2, lambda i: dys.at[:, cols(i)], lambda i: da.at[toks(i)])
+    re_out, re_got = dp_pair(3, lambda i: un.at[toks(i)], lambda i: res_o.at[:, cols(i)])
+    ig_out, ig_got = dp_pair(4, lambda i: un2.at[toks(i)], lambda i: ig_o.at[:, cols(i)])
+    xe_out, xe_got = ex_pair(0, xs, xr)
+    de_out, de_got = ex_pair(1, ds_, dr)
+    rb_out, rb_got = ex_pair(2, rs, rr)
+    sb_out, sb_got = ex_pair(3, ss, sr)
+    xf = pass_pair(4, lambda k: xr.at[rows(k)], lambda k: xp.at[rows(k)])
+    df = pass_pair(5, lambda k: dr.at[rows(k)], lambda k: dp.at[rows(k)])
+
+    def half_pass(no, ref):
+        send, recv = sem_ex.at[2 * no], sem_ex.at[2 * no + 1]
+
+        def out(k):
+            part = ref.at[rows(k), my_half]
+            return copy(part, part, send.at[k], recv.at[k], pm, z)
+
+        def got(k):
+            part = ref.at[rows(k), other_half]
+            return copy(part, part, send.at[k], recv.at[k], pm, z)
+
+        return out, got
+
+    af_out, af_got = half_pass(6, act)
+    ef_out, ef_got = half_pass(7, dga)
+    uf_out, uf_got = half_pass(8, dua)
+    g_out, g_got = q_pair(0, lambda k, i: gs.at[k, i], lambda k, i: gr.at[k, i])
+    h_out, h_got = q_pair(1, lambda k, i: hs.at[k, i], lambda k, i: hr.at[k, i])
+
+    def share_pair(no, ref):
+        def out(k, i):
+            part = ref.at[rows(k), block(q)]
+            return copy(part, part, sem_q.at[2 * no, k, i], sem_q.at[2 * no + 1, k, q], 2 * i + c, z)
+
+        def got(k, i):
+            part = ref.at[rows(k), block(i)]
+            return copy(part, part, sem_q.at[2 * no, k, i], sem_q.at[2 * no + 1, k, i], 2 * i + c, z)
+
+        return out, got
+
+    a_out, a_got = share_pair(2, act)
+    e_out, e_got = share_pair(3, dga)
+    u_out, u_got = share_pair(4, dua)
+    pw = [
+        copy(wg.at[:, other_half], pwg, sem_pw.at[0, 0], sem_pw.at[1, 0], pm, z),
+        copy(wu.at[:, other_half], pwu, sem_pw.at[0, 1], sem_pw.at[1, 1], pm, z),
+        copy(wd.at[other_half], pwd, sem_pw.at[0, 2], sem_pw.at[1, 2], pm, z),
+    ]
+
+    def loop(lo, hi, body):
+        def step(i, carry):
+            body(i)
+            return carry
+
+        lax.fori_loop(lo, hi, step, 0)
+
+    def dp_others(body):
+        loop(1, n, lambda d: body(lax.rem(m + d, n)))
+
+    def ex_others(body):
+        loop(1, e_n, lambda d: body(lax.rem(z + d, e_n)))
+
+    def q_others(body):
+        for d in range(1, q_n):
+            body(lax.rem(q + d, q_n))
+
+    def chunks(body):
+        loop(0, e_n, lambda d: body(d, lax.rem(z + e_n - d, e_n)))
+
+    barrier = pltpu.get_barrier_semaphore()
+    dp_others(lambda i: pl.semaphore_signal(
+        barrier, inc=1, device_id=(i, z), device_id_type=pl.DeviceIdType.MESH))
+    ex_others(lambda i: pl.semaphore_signal(
+        barrier, inc=1, device_id=(m, i), device_id_type=pl.DeviceIdType.MESH))
+    pl.semaphore_wait(barrier, n - 1 + e_n - 1)
+
+    dp_others(lambda i: tg_out(i).start())
+    dp_others(lambda i: xa_out(i).start())
+    for one in pw:
+        one.start()
+    dp_others(lambda i: da_out(i).start())
+    tga[m] = tgt[...]
+    xa[toks(m), :] = tok[:, cols(m)]
+    da[toks(m), :] = dys[:, cols(m)]
+    dp_others(lambda i: tg_got(i).wait_recv())
+    for i in range(n):
+        names = tga[i][0:1, :]
+        place = lax.broadcasted_iota(jnp.int32, (e_n * slots, t_rows), 0)
+        table[:, i * t_rows:(i + 1) * t_rows] = jnp.where(place == names, 1.0, 0.0).astype(BF)
+
+    def slot_out(src, buf, own, out):
+        def one(d):
+            e = lax.rem(z + d, e_n)
+            buf[rows(e), :] = nn(table[rows(e), :], src[...]).astype(BF)
+            out(e).start()
+
+        loop(1, e_n, one)
+        own[rows(z), :] = nn(table[rows(z), :], src[...]).astype(BF)
+
+    dp_others(lambda i: xa_got(i).wait_recv())
+    slot_out(xa, xs, xr, xe_out)
+    dp_others(lambda i: da_got(i).wait_recv())
+    slot_out(da, ds_, dr, de_out)
+    for one in pw:
+        one.wait_recv()
+
+    def gate_up(d, k):
+        @pl.when(d > 0)
+        def _():
+            xe_got(k).wait_recv()
+
+        xf(k).start()
+        xf(k).wait_recv()
+        for at, own_w, other_w in ((0, wg, pwg), (1, wu, pwu)):
+            part = nn(xr[rows(k), :], own_w[:, my_half]) + nn(xp[rows(k), :], other_w[...])
+            part = part.astype(BF)
+            for i in range(q_n):
+                gs[k, i, :, at * b:(at + 1) * b] = part[:, i * b:(i + 1) * b]
+        q_others(lambda i: g_out(k, i).start())
+
+    chunks(gate_up)
+
+    def activate(d, k):
+        total = gs[k, q].astype(F32)
+        for dd in range(1, q_n):
+            i = lax.rem(q + dd, q_n)
+            g_got(k, i).wait_recv()
+            total = total + gr[k, i].astype(F32)
+        gate, up = total[:, :b], total[:, b:]
+        pre[rows(k), :] = gate
+        upv[rows(k), :] = up
+        act[rows(k), block(q)] = (gate * jax.nn.sigmoid(gate) * up).astype(BF)
+        q_others(lambda i: a_out(k, i).start())
+
+    chunks(activate)
+
+    def down(d, k):
+        q_others(lambda i: a_got(k, i).wait_recv())
+        af_out(k).start()
+
+        @pl.when(d > 0)
+        def _():
+            de_got(k).wait_recv()
+
+        df(k).start()
+        df(k).wait_recv()
+        part = nt(dr[rows(k), :], wd[my_half, :]) + nt(dp[rows(k), :], pwd[...])
+        part = part.astype(BF)
+        for i in range(q_n):
+            hs[k, i] = part[:, i * b:(i + 1) * b]
+        q_others(lambda i: h_out(k, i).start())
+        af_got(k).wait_recv()
+        result = nn(act[rows(k), :], wd[...]).astype(BF)
+
+        @pl.when(d == 0)
+        def _():
+            rr[rows(k), :] = result
+
+        @pl.when(d > 0)
+        def _():
+            rs[rows(k), :] = result
+            rb_out(k).start()
+
+    chunks(down)
+
+    def act_grad(d, k):
+        total = hs[k, q].astype(F32)
+        for dd in range(1, q_n):
+            i = lax.rem(q + dd, q_n)
+            h_got(k, i).wait_recv()
+            total = total + hr[k, i].astype(F32)
+        gate, up = pre[rows(k), :], upv[rows(k), :]
+        sig = jax.nn.sigmoid(gate)
+        dga[rows(k), block(q)] = (total * up * sig * (1.0 + gate * (1.0 - sig))).astype(BF)
+        dua[rows(k), block(q)] = (total * gate * sig).astype(BF)
+        q_others(lambda i: e_out(k, i).start())
+        q_others(lambda i: u_out(k, i).start())
+
+    chunks(act_grad)
+
+    x_t[...] = xr[...].T
+    tile = 2 * b
+
+    def down_grad(j):
+        at = pl.ds(pl.multiple_of(j * tile, 128), tile)
+        gd_o[at, :] = tn(act[:, at], dr[...]).astype(BF)
+
+    loop(0, ff // tile, down_grad)
+
+    def handed(d, k):
+        q_others(lambda i: e_got(k, i).wait_recv())
+        ef_out(k).start()
+        q_others(lambda i: u_got(k, i).wait_recv())
+        uf_out(k).start()
+
+    chunks(handed)
+
+    def input_grad(d, k):
+        ef_got(k).wait_recv()
+        uf_got(k).wait_recv()
+        value = (nt(dga[rows(k), :], wg[...]) + nt(dua[rows(k), :], wu[...])).astype(BF)
+
+        @pl.when(d == 0)
+        def _():
+            sr[rows(k), :] = value
+
+        @pl.when(d > 0)
+        def _():
+            ss[rows(k), :] = value
+            sb_out(k).start()
+
+    chunks(input_grad)
+
+    def give_back(src, buf, out):
+        def one(d):
+            i = lax.rem(m + d, n)
+            buf[toks(i), :] = tn(table[:, toks(i)], src[...]).astype(BF)
+            out(i).start()
+
+        loop(1, n, one)
+        buf[toks(m), :] = tn(table[:, toks(m)], src[...]).astype(BF)
+
+    ex_others(lambda i: rb_got(i).wait_recv())
+    give_back(rr, un, re_out)
+    res_o[:, cols(m)] = un[toks(m), :]
+
+    def weight_grad(j):
+        at = pl.ds(pl.multiple_of(j * tile, 128), tile)
+        gg_o[:, at] = nn(x_t[...], dga[:, at]).astype(BF)
+        gu_o[:, at] = nn(x_t[...], dua[:, at]).astype(BF)
+
+    loop(0, ff // tile, weight_grad)
+    ex_others(lambda i: sb_got(i).wait_recv())
+    give_back(sr, un2, ig_out)
+    ig_o[:, cols(m)] = un2[toks(m), :]
+
+    def dp_end(i):
+        re_got(i).wait_recv()
+        ig_got(i).wait_recv()
+        for out in (tg_out, xa_out, da_out, re_out, ig_out):
+            out(i).wait_send()
+
+    dp_others(dp_end)
+
+    def ex_end(i):
+        for out in (xe_out, de_out, rb_out, sb_out):
+            out(i).wait_send()
+
+    ex_others(ex_end)
+    for one in pw:
+        one.wait_send()
+
+    def chunk_end(k):
+        for out in (xf, df, af_out, ef_out, uf_out):
+            out(k).wait_send()
+        for out in (g_out, h_out, a_out, e_out, u_out):
+            q_others(lambda i: out(k, i).wait_send())
+
+    loop(0, e_n, chunk_end)
+
+
+def fused_layer(tokens, probs, routes, w_gate, w_up, w_down, cotangent, n, e_n, cap):
+    t_rows, width = tokens.shape
+    w = width // n
+    ff = w_gate.shape[2]
+    slots, fh, q_n = n * cap, ff // 2, n // 2
+    b = fh // q_n
+    r = e_n * slots
+    weight = probs.astype(F32)
+    dys = (cotangent.astype(F32) * weight).astype(BF)
+    flat = routes.reshape(-1)
+    hits = (flat[:, None] == jnp.arange(e_n, dtype=jnp.int32)[None, :]).astype(jnp.int32)
+    before = jnp.cumsum(hits, axis=0) - hits
+    place = jnp.sum(before * hits, axis=1)
+    target = flat * slots + lax.axis_index("dp").astype(jnp.int32) * cap + place
+    tgt = jnp.broadcast_to(target[None, :], (8, t_rows))
+    vm = pl.BlockSpec(memory_space=pltpu.VMEM)
+
+    def v(*shape, dtype=BF):
+        return pltpu.VMEM(shape, dtype)
+
+    scratch = [
+        v(n, 8, t_rows, dtype=jnp.int32), v(r, n * t_rows),
+        v(n * t_rows, w), v(n * t_rows, w),
+        v(r, w), v(r, w), v(r, w), v(r, w), v(r, w), v(r, w),
+        v(w, fh), v(w, fh), v(fh, w),
+        v(e_n, q_n, slots, 2 * b), v(e_n, q_n, slots, 2 * b),
+        v(e_n, q_n, slots, b), v(e_n, q_n, slots, b),
+        v(r, b, dtype=F32), v(r, b, dtype=F32),
+        v(r, ff), v(r, ff), v(r, ff),
+        v(r, w), v(r, w), v(r, w), v(r, w),
+        v(n * t_rows, w), v(n * t_rows, w), v(w, r),
+        pltpu.SemaphoreType.DMA((10, n)),
+        pltpu.SemaphoreType.DMA((2, 3)),
+        pltpu.SemaphoreType.DMA((18, e_n)),
+        pltpu.SemaphoreType.DMA((10, e_n, q_n)),
+    ]
+    result, input_grad, gg, gu, gd = pl.pallas_call(
+        functools.partial(layer_kernel, n, e_n, cap),
+        out_shape=(
+            jax.ShapeDtypeStruct((t_rows, width), BF),
+            jax.ShapeDtypeStruct((t_rows, width), BF),
+            jax.ShapeDtypeStruct((w, ff), BF),
+            jax.ShapeDtypeStruct((w, ff), BF),
+            jax.ShapeDtypeStruct((ff, w), BF),
+        ),
+        in_specs=[vm] * 6,
+        out_specs=(vm,) * 5,
+        scratch_shapes=scratch,
+        compiler_params=pltpu.CompilerParams(
+            collective_id=0, has_side_effects=True, vmem_limit_bytes=62 * 1024 * 1024
+        ),
+    )(tokens, dys, tgt, w_gate[0], w_up[0], w_down[0])
+    mixed = (result.astype(F32) * weight).astype(BF)
+    return mixed, input_grad, gg[None], gu[None], gd[None]
 
 
 def slot_table(routes, experts_all, capacity):
@@ -48,6 +460,14 @@
     tok_rows, width = tokens.shape
     top = routes.shape[1]
     capacity = max(2, 17 * tok_rows * top // (16 * experts_all))
+    ff = w_gate.shape[2]
+    if (
+        local_count == 1 and top == 1 and n_dp % 2 == 0 and ff % (n_dp * 128) == 0
+        and tok_rows % 128 == 0 and width % (n_dp * 128) == 0 and (n_dp * capacity) % 16 == 0
+    ):
+        return fused_layer(
+            tokens, probs, routes, w_gate, w_up, w_down, cotangent, n_dp, n_exp, capacity
+        )
     blocks = n_dp * n_exp
     slot_width = width // n_dp
     table = slot_table(routes, experts_all, capacity)

time: 327 us -> 177 us (0.54)
  the two profiles are of different devices: /device:TPU:25 before, /device:TPU:1 now
where the time goes in v1:
time: 177 us
  Pallas kernels  162 us (92%)
  other arithmetic  8.05 us (5%)
  local copies, waits for them, and re-layouts  6.38 us (4%)
    pallas_call x1, Pallas kernels, fused_layer(): pl.pallas_call(functools.partial(layer_kernel, n, e_n, cap), out_shape=(j...  162 us
    unnamed x12, local copies, waits for them, and re-layouts  5.78 us

profile of v1, /device:TPU:1, one launch (start us, length us, event | category | flops | bytes accessed | tf_op | source)
XLA Modules:
  0.0 176.8 jit_solution(6552760885437732125)
XLA Ops:
  0.6 0.7 bitcast_convert_fusion
  1.3 0.7 fusion
  2.0 0.2 reduce_window_sum.11
  2.2 0.8 select_reduce_fusion
  3.0 0.7 add_add_fusion
  3.7 0.6 broadcast_in_dim.16.tgt
  4.3 2.5 %multiply_convert_fusion.1.dys = bf16[128,4096]{1,0:T(8,128)(2,1)} fusion(bf16[128,4096]{1,0:T(8,128)(2,1)} %param.13, f32[128]{0:T(128)S(1)} %bitcast_convert_fusion), kind=kLoop, calls=%fused_computation.1 | loop fusion | flops 1572864 | bytes 2097664 | tf_op jit(solution)/shard_map/convert_element_type | solution.py:371
  6.8 161.7 %shard_map.110 = (bf16[128,4096]{1,0:T(8,128)(2,1)}, bf16[128,4096]{1,0:T(8,128)(2,1)}, bf16[512,1024]{1,0:T(8,128)(2,1)}, bf16[512,1024]{1,0:T(8,128)(2,1)}, bf16[1024,512]{1,0:T(8,128)(2,1)}) custom-call(bf16[128,4096]{1,0:T(8,128)(2,1)} %tok.1, bf16[128,4096]{1,0:T(8,128)(2,1)} %multiply_convert_fusion.1.dys, s32[8,128]{1,0:T(8,128)} %broadcast_in_dim.16.tgt, ...), custom_call_target="tpu_custom_call" | custom-call | tf_op jit(solution)/shard_map/pallas_call | solution.py:399
  168.5 0.0 copy-start.3
  168.5 2.5 %multiply_convert_fusion = bf16[128,4096]{1,0:T(8,128)(2,1)} fusion(bf16[128,4096]{1,0:T(8,128)(2,1)} %get-tuple-element.10, f32[128]{0:T(128)S(1)} %bitcast_convert_fusion), kind=kLoop, calls=%fused_computation | loop fusion | flops 1572864 | bytes 2097664 | tf_op jit(solution)/shard_map/convert_element_type | solution.py:415
  171.1 0.0 copy-done.3
  171.1 0.0 copy-start.2
  171.1 1.0 copy.16
  172.0 0.6 copy-done.2
  172.7 0.0 copy-start.1
  172.7 1.0 copy.17
  173.6 0.6 copy-done.1
  174.3 0.0 copy-start
  174.3 1.0 copy.18
  175.2 0.6 copy-done
  175.9 1.0 copy.19
Async XLA Ops:
  168.5 2.6 %copy-start.3 = (bf16[128,4096]{1,0:T(8,128)(2,1)S(1)}, bf16[128,4096]{1,0:T(8,128)(2,1)}, u32[]{:S(2)}) copy-start(bf16[128,4096]{1,0:T(8,128)(2,1)} %get-tuple-element.21) | copy-start | bytes 3145732
  171.1 1.6 copy-start.2
  172.7 1.6 copy-start.1
  174.3 1.6 copy-start

commit v2 on v1

--- a/solution.py
+++ b/solution.py
@@ -25,10 +25,10 @@
 
 def layer_kernel(
     n, e_n, cap,
-    tok, dys, tgt, wg, wu, wd,
+    tok, cot, tgt, wt, wg, wu, wd,
     res_o, ig_o, gg_o, gu_o, gd_o,
     tga, table, xa, da, xs, ds_, xr, dr, xp, dp, pwg, pwu, pwd,
-    gs, gr, hs, hr, pre, upv, act, dga, dua, rs, rr, ss, sr, un, un2, x_t,
+    gs, gr, hs, hr, pre, upv, act, dga, dua, rs, rr, ss, sr, un, un2, x_t, dys,
     sem_dp, sem_pw, sem_ex, sem_q,
 ):
     m = lax.axis_index("dp")
@@ -155,18 +155,44 @@
 
         lax.fori_loop(lo, hi, step, 0)
 
+    def partner(at, d, size):
+        if size & (size - 1):
+            return lax.rem(at + d, size)
+        other, step = at, 1
+        while step < size:
+            if d & step:
+                other = other + step - 2 * step * lax.rem(at // step, 2)
+            step *= 2
+        return other
+
     def dp_others(body):
-        loop(1, n, lambda d: body(lax.rem(m + d, n)))
+        for d in range(1, n):
+            body(partner(m, d, n))
 
     def ex_others(body):
         loop(1, e_n, lambda d: body(lax.rem(z + d, e_n)))
 
     def q_others(body):
         for d in range(1, q_n):
-            body(lax.rem(q + d, q_n))
+            body(partner(q, d, q_n))
 
     def chunks(body):
         loop(0, e_n, lambda d: body(d, lax.rem(z + e_n - d, e_n)))
+
+    def far_first(body):
+        loop(1, e_n + 1, lambda d: body(d, lax.rem(z + 2 * e_n - d, e_n)))
+
+    def ahead(first, then):
+        def step(d):
+            @pl.when(d <= e_n)
+            def _():
+                first(lax.rem(z + 2 * e_n - d, e_n))
+
+            @pl.when(d > 1)
+            def _():
+                then(d - 1, lax.rem(z + 2 * e_n - (d - 1), e_n))
+
+        loop(1, e_n + 2, step)
 
     barrier = pltpu.get_barrier_semaphore()
     dp_others(lambda i: pl.semaphore_signal(
@@ -179,6 +205,10 @@
     dp_others(lambda i: xa_out(i).start())
     for one in pw:
         one.start()
+    wide = tok.shape[1] // 8
+    for i in range(8):
+        at = slice(i * wide, (i + 1) * wide)
+        dys[:, at] = (cot[:, at].astype(F32) * wt[...]).astype(BF)
     dp_others(lambda i: da_out(i).start())
     tga[m] = tgt[...]
     xa[toks(m), :] = tok[:, cols(m)]
@@ -224,7 +254,7 @@
     def activate(d, k):
         total = gs[k, q].astype(F32)
         for dd in range(1, q_n):
-            i = lax.rem(q + dd, q_n)
+            i = partner(q, dd, q_n)
             g_got(k, i).wait_recv()
             total = total + gr[k, i].astype(F32)
         gate, up = total[:, :b], total[:, b:]
@@ -233,12 +263,9 @@
         act[rows(k), block(q)] = (gate * jax.nn.sigmoid(gate) * up).astype(BF)
         q_others(lambda i: a_out(k, i).start())
 
-    chunks(activate)
+    far_first(activate)
 
     def down(d, k):
-        q_others(lambda i: a_got(k, i).wait_recv())
-        af_out(k).start()
-
         @pl.when(d > 0)
         def _():
             de_got(k).wait_recv()
@@ -250,24 +277,32 @@
         for i in range(q_n):
             hs[k, i] = part[:, i * b:(i + 1) * b]
         q_others(lambda i: h_out(k, i).start())
+
+    chunks(down)
+
+    def act_pass(k):
+        q_others(lambda i: a_got(k, i).wait_recv())
+        af_out(k).start()
+
+    def result_rows(d, k):
         af_got(k).wait_recv()
         result = nn(act[rows(k), :], wd[...]).astype(BF)
 
-        @pl.when(d == 0)
+        @pl.when(d == e_n)
         def _():
             rr[rows(k), :] = result
 
-        @pl.when(d > 0)
+        @pl.when(d < e_n)
         def _():
             rs[rows(k), :] = result
             rb_out(k).start()
 
-    chunks(down)
+    ahead(act_pass, result_rows)
 
     def act_grad(d, k):
         total = hs[k, q].astype(F32)
         for dd in range(1, q_n):
-            i = lax.rem(q + dd, q_n)
+            i = partner(q, dd, q_n)
             h_got(k, i).wait_recv()
             total = total + hr[k, i].astype(F32)
         gate, up = pre[rows(k), :], upv[rows(k), :]
@@ -277,48 +312,47 @@
         q_others(lambda i: e_out(k, i).start())
         q_others(lambda i: u_out(k, i).start())
 
-    chunks(act_grad)
-
-    x_t[...] = xr[...].T
-    tile = 2 * b
-
-    def down_grad(j):
-        at = pl.ds(pl.multiple_of(j * tile, 128), tile)
-        gd_o[at, :] = tn(act[:, at], dr[...]).astype(BF)
-
-    loop(0, ff // tile, down_grad)
-
-    def handed(d, k):
+    far_first(act_grad)
+
+    def handed(k):
         q_others(lambda i: e_got(k, i).wait_recv())
         ef_out(k).start()
         q_others(lambda i: u_got(k, i).wait_recv())
         uf_out(k).start()
 
-    chunks(handed)
-
     def input_grad(d, k):
         ef_got(k).wait_recv()
         uf_got(k).wait_recv()
         value = (nt(dga[rows(k), :], wg[...]) + nt(dua[rows(k), :], wu[...])).astype(BF)
 
-        @pl.when(d == 0)
+        @pl.when(d == e_n)
         def _():
             sr[rows(k), :] = value
 
-        @pl.when(d > 0)
+        @pl.when(d < e_n)
         def _():
             ss[rows(k), :] = value
             sb_out(k).start()
 
-    chunks(input_grad)
+    ahead(handed, input_grad)
+
+    x_t[...] = xr[...].T
+    tile = 2 * b
+
+    def down_grad(j):
+        at = pl.ds(pl.multiple_of(j * tile, 128), tile)
+        gd_o[at, :] = tn(act[:, at], dr[...]).astype(BF)
+
+    loop(0, ff // tile, down_grad)
 
     def give_back(src, buf, out):
         def one(d):
-            i = lax.rem(m + d, n)
+            i = partner(m, d, n)
             buf[toks(i), :] = tn(table[:, toks(i)], src[...]).astype(BF)
             out(i).start()
 
-        loop(1, n, one)
+        for d in range(1, n):
+            one(d)
         buf[toks(m), :] = tn(table[:, toks(m)], src[...]).astype(BF)
 
     ex_others(lambda i: rb_got(i).wait_recv())
@@ -368,7 +402,6 @@
     b = fh // q_n
     r = e_n * slots
     weight = probs.astype(F32)
-    dys = (cotangent.astype(F32) * weight).astype(BF)
     flat = routes.reshape(-1)
     hits = (flat[:, None] == jnp.arange(e_n, dtype=jnp.int32)[None, :]).astype(jnp.int32)
     before = jnp.cumsum(hits, axis=0) - hits
@@ -390,7 +423,7 @@
         v(r, b, dtype=F32), v(r, b, dtype=F32),
         v(r, ff), v(r, ff), v(r, ff),
         v(r, w), v(r, w), v(r, w), v(r, w),
-        v(n * t_rows, w), v(n * t_rows, w), v(w, r),
+        v(n * t_rows, w), v(n * t_rows, w), v(w, r), v(t_rows, width),
         pltpu.SemaphoreType.DMA((10, n)),
         pltpu.SemaphoreType.DMA((2, 3)),
         pltpu.SemaphoreType.DMA((18, e_n)),
@@ -405,13 +438,13 @@
             jax.ShapeDtypeStruct((w, ff), BF),
             jax.ShapeDtypeStruct((ff, w), BF),
         ),
-        in_specs=[vm] * 6,
+        in_specs=[vm] * 7,
         out_specs=(vm,) * 5,
         scratch_shapes=scratch,
         compiler_params=pltpu.CompilerParams(
             collective_id=0, has_side_effects=True, vmem_limit_bytes=62 * 1024 * 1024
         ),
-    )(tokens, dys, tgt, w_gate[0], w_up[0], w_down[0])
+    )(tokens, cotangent, tgt, weight, w_gate[0], w_up[0], w_down[0])
     mixed = (result.astype(F32) * weight).astype(BF)
     return mixed, input_grad, gg[None], gu[None], gd[None]
 

time: 177 us -> 171 us (0.966)
  the two profiles are of different devices: /device:TPU:1 before, /device:TPU:25 now
where the time goes in v2:
time: 171 us
  Pallas kernels  157 us (92%)
  local copies, waits for them, and re-layouts  7.16 us (4%)
  other arithmetic  5.69 us (3%)
    pallas_call x1, Pallas kernels, fused_layer(): pl.pallas_call(functools.partial(layer_kernel, n, e_n, cap), out_shape=(j...  157 us
    unnamed x13, local copies, waits for them, and re-layouts  6.57 us

profile of v2, /device:TPU:25, one launch (start us, length us, event | category | flops | bytes accessed | tf_op | source)
XLA Modules:
  0.0 170.9 jit_solution(2535822373486893049)
XLA Ops:
  0.6 0.8 copy.13
  1.4 0.1 convert_reduce_fusion
  1.5 0.6 convert_element_type.13.wt
  2.2 0.7 fusion
  2.9 0.2 reduce_window_sum.11
  3.1 0.8 select_reduce_fusion
  3.9 0.7 add_add_fusion
  4.6 0.6 broadcast_in_dim.16.tgt
  5.2 157.3 %shard_map.110 = (bf16[128,4096]{1,0:T(8,128)(2,1)}, bf16[128,4096]{1,0:T(8,128)(2,1)}, bf16[512,1024]{1,0:T(8,128)(2,1)}, bf16[512,1024]{1,0:T(8,128)(2,1)}, bf16[1024,512]{1,0:T(8,128)(2,1)}) custom-call(bf16[128,4096]{1,0:T(8,128)(2,1)} %tok.1, bf16[128,4096]{1,0:T(8,128)(2,1)} %cot.1, s32[8,128]{1,0:T(8,128)} %broadcast_in_dim.16.tgt, ...), custom_call_target="tpu_custom_call" | custom-call | tf_op jit(solution)/shard_map/pallas_call | solution.py:432
  162.5 0.0 copy-start.3
  162.6 2.5 %multiply_convert_fusion = bf16[128,4096]{1,0:T(8,128)(2,1)} fusion(bf16[128,4096]{1,0:T(8,128)(2,1)} %get-tuple-element.10, f32[128]{0:T(128)S(1)} %convert_reduce_fusion), kind=kLoop, calls=%fused_computation | loop fusion | flops 1572864 | bytes 2097664 | tf_op jit(solution)/shard_map/convert_element_type | solution.py:448
  165.1 0.0 copy-done.3
  165.1 0.0 copy-start.2
  165.1 1.0 copy.18
  166.1 0.6 copy-done.2
  166.7 0.0 copy-start.1
  166.7 1.0 copy.19
  167.7 0.6 copy-done.1
  168.3 0.0 copy-start
  168.3 1.0 copy.20
  169.3 0.6 copy-done
  169.9 1.0 copy.21
Async XLA Ops:
  162.5 2.6 %copy-start.3 = (bf16[128,4096]{1,0:T(8,128)(2,1)S(1)}, bf16[128,4096]{1,0:T(8,128)(2,1)}, u32[]{:S(2)}) copy-start(bf16[128,4096]{1,0:T(8,128)(2,1)} %get-tuple-element.21) | copy-start | bytes 3145732
  165.1 1.6 copy-start.2
  166.7 1.6 copy-start.1
  168.3 1.6 copy-start

commit v3 on v2

--- a/solution.py
+++ b/solution.py
@@ -25,11 +25,11 @@
 
 def layer_kernel(
     n, e_n, cap,
-    tok, cot, tgt, wt, wg, wu, wd,
+    tok, cot, tgt, wt, wg_h, wu_h, wd_h,
     res_o, ig_o, gg_o, gu_o, gd_o,
     tga, table, xa, da, xs, ds_, xr, dr, xp, dp, pwg, pwu, pwd,
-    gs, gr, hs, hr, pre, upv, act, dga, dua, rs, rr, ss, sr, un, un2, x_t, dys,
-    sem_dp, sem_pw, sem_ex, sem_q,
+    gs, gr, hs, hr, pre, upv, act, dga, dua, rs, rr, ss, sr, un, un2, x_t, dys, wg, wu, wd,
+    sem_own, sem_dp, sem_pw, sem_ex, sem_q,
 ):
     m = lax.axis_index("dp")
     z = lax.axis_index("expert")
@@ -39,7 +39,7 @@
     pm = m + 1 - 2 * c
     slots = n * cap
     t_rows, w = tok.shape[0], tok.shape[1] // n
-    ff = wg.shape[1]
+    ff = wg_h.shape[1]
     fh = ff // 2
     b = fh // q_n
 
@@ -143,9 +143,9 @@
     e_out, e_got = share_pair(3, dga)
     u_out, u_got = share_pair(4, dua)
     pw = [
-        copy(wg.at[:, other_half], pwg, sem_pw.at[0, 0], sem_pw.at[1, 0], pm, z),
-        copy(wu.at[:, other_half], pwu, sem_pw.at[0, 1], sem_pw.at[1, 1], pm, z),
-        copy(wd.at[other_half], pwd, sem_pw.at[0, 2], sem_pw.at[1, 2], pm, z),
+        copy(wg_h.at[:, other_half], pwg, sem_pw.at[0, 0], sem_pw.at[1, 0], pm, z),
+        copy(wu_h.at[:, other_half], pwu, sem_pw.at[0, 1], sem_pw.at[1, 1], pm, z),
+        copy(wd_h.at[other_half], pwd, sem_pw.at[0, 2], sem_pw.at[1, 2], pm, z),
     ]
 
     def loop(lo, hi, body):
@@ -194,6 +194,12 @@
 
         loop(1, e_n + 2, step)
 
+    own = [
+        pltpu.make_async_copy(src, dst, sem_own.at[i])
+        for i, (src, dst) in enumerate(((wg_h, wg), (wu_h, wu), (wd_h, wd)))
+    ]
+    for one in own:
+        one.start()
     barrier = pltpu.get_barrier_semaphore()
     dp_others(lambda i: pl.semaphore_signal(
         barrier, inc=1, device_id=(i, z), device_id_type=pl.DeviceIdType.MESH))
@@ -232,6 +238,8 @@
     slot_out(xa, xs, xr, xe_out)
     dp_others(lambda i: da_got(i).wait_recv())
     slot_out(da, ds_, dr, de_out)
+    for one in own:
+        one.wait()
     for one in pw:
         one.wait_recv()
 
@@ -423,7 +431,8 @@
         v(r, b, dtype=F32), v(r, b, dtype=F32),
         v(r, ff), v(r, ff), v(r, ff),
         v(r, w), v(r, w), v(r, w), v(r, w),
-        v(n * t_rows, w), v(n * t_rows, w), v(w, r), v(t_rows, width),
+        v(n * t_rows, w), v(n * t_rows, w), v(w, r), v(t_rows, width), v(w, ff), v(w, ff), v(ff, w),
+        pltpu.SemaphoreType.DMA((3,)),
         pltpu.SemaphoreType.DMA((10, n)),
         pltpu.SemaphoreType.DMA((2, 3)),
         pltpu.SemaphoreType.DMA((18, e_n)),
@@ -438,7 +447,7 @@
             jax.ShapeDtypeStruct((w, ff), BF),
             jax.ShapeDtypeStruct((ff, w), BF),
         ),
-        in_specs=[vm] * 7,
+        in_specs=[vm] * 4 + [pl.BlockSpec(memory_space=pl.ANY)] * 3,
         out_specs=(vm,) * 5,
         scratch_shapes=scratch,
         compiler_params=pltpu.CompilerParams(

time: 171 us -> 170 us (level)
  no operation moved by 1% of the time
where the time goes in v3:
time: 170 us
  Pallas kernels  156 us (92%)
  local copies, waits for them, and re-layouts  7.16 us (4%)
  other arithmetic  5.69 us (3%)
    pallas_call x1, Pallas kernels, fused_layer(): pl.pallas_call(functools.partial(layer_kernel, n, e_n, cap), out_shape=(j...  156 us
    unnamed x13, local copies, waits for them, and re-layouts  6.57 us

profile of v3, /device:TPU:25, one launch (start us, length us, event | category | flops | bytes accessed | tf_op | source)
XLA Modules:
  0.0 170.0 jit_solution(2689379588704110511)
XLA Ops:
  0.6 0.8 copy.13
  1.4 0.1 convert_reduce_fusion
  1.5 0.6 convert_element_type.13.wt
  2.2 0.7 fusion
  2.9 0.2 reduce_window_sum.11
  3.1 0.8 select_reduce_fusion
  3.9 0.7 add_add_fusion
  4.6 0.6 broadcast_in_dim.16.tgt
  5.2 156.4 %shard_map.110 = (bf16[128,4096]{1,0:T(8,128)(2,1)}, bf16[128,4096]{1,0:T(8,128)(2,1)}, bf16[512,1024]{1,0:T(8,128)(2,1)}, bf16[512,1024]{1,0:T(8,128)(2,1)}, bf16[1024,512]{1,0:T(8,128)(2,1)}) custom-call(bf16[128,4096]{1,0:T(8,128)(2,1)} %tok.1, bf16[128,4096]{1,0:T(8,128)(2,1)} %cot.1, s32[8,128]{1,0:T(8,128)} %broadcast_in_dim.16.tgt, ...), custom_call_target="tpu_custom_call" | custom-call | tf_op jit(solution)/shard_map/pallas_call | solution.py:441
  161.6 0.0 copy-start.3
  161.6 2.5 %multiply_convert_fusion = bf16[128,4096]{1,0:T(8,128)(2,1)} fusion(bf16[128,4096]{1,0:T(8,128)(2,1)} %get-tuple-element.10, f32[128]{0:T(128)S(1)} %convert_reduce_fusion), kind=kLoop, calls=%fused_computation | loop fusion | flops 1572864 | bytes 2097664 | tf_op jit(solution)/shard_map/convert_element_type | solution.py:457
  164.2 0.0 copy-done.3
  164.2 0.0 copy-start.2
  164.2 1.0 copy.18
  165.1 0.6 copy-done.2
  165.8 0.0 copy-start.1
  165.8 1.0 copy.19
  166.7 0.6 copy-done.1
  167.4 0.0 copy-start
  167.4 1.0 copy.20
  168.3 0.6 copy-done
  169.0 1.0 copy.21
Async XLA Ops:
  161.6 2.6 %copy-start.3 = (bf16[128,4096]{1,0:T(8,128)(2,1)S(1)}, bf16[128,4096]{1,0:T(8,128)(2,1)}, u32[]{:S(2)}) copy-start(bf16[128,4096]{1,0:T(8,128)(2,1)} %get-tuple-element.21) | copy-start | bytes 3145732
  164.2 1.6 copy-start.2
  165.8 1.6 copy-start.1
  167.4 1.6 copy-start
